TPU v7x, 768 devices: a whole 4x8x12 slice. The times are simulated.
768 devices in a mesh: cond: 16 (over x, y_lo, core), slab: 48 (over z, y_hi).
Axes of the slice: x: 4, y: 8 (y_hi: 4, y_lo: 2; y = y_hi * 2 + y_lo), z: 12, core: 2. Of those that a mesh axis runs over, the one named last changes fastest.
Arguments:
- adjoint: float32 [16, 192, 512, 128], P('cond', 'slab'), may hold values from -6 to 6
- phase: bfloat16 [16, 192, 512, 128], P('cond', 'slab'), may hold values from -1.09375 to 1.09375
- targets: bfloat16 [16, 1536, 128], P('cond', 'slab'), may hold values from -1 to 1
- owners: int32 [16, 1536, 1], P('cond', 'slab'), may hold values from 0 to 47; in each aligned block of 32 rows (0 to 31, 32 to 63, ..., all dimensions but the last counted through in order) at most 2 rows name the same one
- target_cell: int32 [16, 1536], P('cond', 'slab'), may hold values from 0 to 2047
- rate_index: int32 [16], P('cond'), may hold values from 0 to 7
- inflow_rates: float32 [8], replicated, may hold values from 0.5 to 2
- wall_mask: int32 [2, 192, 512], P(None, 'slab'), may hold values 0 or 1
Outputs:
- adjoint_out: float32 [16, 192, 512, 128], P('cond', 'slab')
- wall_gradient: float32 [2, 192, 512], P(None, 'slab')
Inputs may be any that keep to these rules, and one draw needn't show every extreme that they name: `owners`: within each aligned block of 32 rows, no slab is named by more than 2 rows.
All inputs are finite; a program needn't handle non-finite values. No bound on the sum of `wall_mask` on one device may be relied on, other than what follows from the above.
Results may differ from a plain program's by a relative error of at most 0.0003.
Values may be sent and summed in bfloat16 or wider, within the bound.
A program may use at most 32 MiB of HBM per device.

v0:
```python
import jax
import jax.numpy as jnp
from jax import lax
from jax.sharding import PartitionSpec as P

mobility_step = 0.02
stiffness_step = 0.01
transport_step = 0.125
wall_weight = 0.25


def extended_2(cells, sides, width):
    for axis, dim in sides:
        count = lax.axis_size(axis)
        ends = count - 1
        head = lax.slice_in_dim(cells, 0, width, axis=dim)
        tail = lax.slice_in_dim(cells, cells.shape[dim] - width, cells.shape[dim], axis=dim)
        cells = jnp.concatenate(
            [
                lax.ppermute(tail, axis, [(i, (i + 1) % count) for i in range(ends)]),
                cells,
                lax.ppermute(head, axis, [((i + 1) % count, i) for i in range(ends)]),
            ],
            axis=dim,
        )
    return cells


def inner_laplacian(field):
    center = field[1:-1]
    along_y = jnp.pad(center, ((0, 0), (1, 1), (0, 0)))
    along_z = jnp.pad(center, ((0, 0), (0, 0), (1, 1)))
    return (
        field[2:]
        + field[:-2]
        + along_y[:, 2:]
        + along_y[:, :-2]
        + along_z[:, :, 2:]
        + along_z[:, :, :-2]
        - 6.0 * center
    )


def within_grid(length, first_row, grid_rows):
    placed = first_row + jnp.arange(length)
    within = (placed >= 0) & (placed < grid_rows)
    return within.astype(jnp.float32)[:, None, None]


def adjoint_step(extended, curvature, inflow, first_row, grid_rows):
    length = extended.shape[0]
    first_lap = inner_laplacian(extended) * within_grid(length - 2, first_row + 1, grid_rows)
    second_lap = inner_laplacian(first_lap)
    center = extended[2:-2]
    column_depth = extended.shape[2]
    height = (jnp.arange(column_depth).astype(jnp.float32) + 0.5) / column_depth
    profile = 4.0 * height * (1.0 - height)
    padded = jnp.pad(center, ((0, 0), (1, 1), (0, 0)))
    transport = (padded[:, 2:] - padded[:, :-2]) * profile
    updated = (
        center
        + mobility_step * curvature * first_lap[1:-1]
        - stiffness_step * second_lap
        + transport_step * inflow * transport
    )
    return updated * within_grid(length - 4, first_row + 2, grid_rows)


def wall_term(state, phase32, wall_mask):
    lower_wall = (1.0 - phase32[:, :, 0] ** 2) * state[:, :, 0]
    upper_wall = (1.0 - phase32[:, :, -1] ** 2) * state[:, :, -1]
    return wall_weight * wall_mask.astype(jnp.float32) * jnp.stack([lower_wall, upper_wall])


def inject(state, flat_phase, arrived, row_index):
    cells_here = flat_phase.shape[0]
    safe_index = jnp.minimum(row_index, cells_here - 1)
    source = flat_phase[safe_index] - arrived.astype(jnp.float32)
    shaped = state.reshape(cells_here, state.shape[2])
    return shaped.at[row_index].add(source, mode="drop").reshape(state.shape)


def on_device(adjoint, phase, targets, owners, target_cell, rate_index, inflow_rates, wall_mask):
    state = adjoint[0]
    phase32 = phase[0].astype(jnp.float32)
    slab_width = state.shape[0]
    column_depth = state.shape[2]
    slab_count = lax.axis_size("slab")
    position = lax.axis_index("slab")
    grid_rows = slab_width * slab_count
    anchor = position * slab_width
    choose = jnp.arange(inflow_rates.shape[0]) == rate_index[0]
    inflow = jnp.sum(jnp.where(choose, inflow_rates, 0.0))
    curvature = 3.0 * phase32 * phase32 - 1.0
    gradient = jnp.zeros(wall_mask.shape, jnp.float32)
    for sweep in range(2):
        extended = extended_2(state, (("slab", 0),), 2)
        state = adjoint_step(extended, curvature, inflow, anchor - 2, grid_rows)
        gradient = gradient + wall_term(state, phase32, wall_mask)
    flat_phase = phase32.reshape(-1, column_depth)
    cells_here = flat_phase.shape[0]
    gathered_rows, gathered_cells, gathered_owners = (
        lax.all_gather(targets, "slab", axis=1, tiled=True),
        lax.all_gather(target_cell, "slab", axis=1, tiled=True),
        lax.all_gather(owners, "slab", axis=1, tiled=True),
    )
    row_index = jnp.where(gathered_owners[0, :, 0] == position, gathered_cells[0], cells_here)
    state = inject(state, flat_phase, gathered_rows[0], row_index)
    wall_gradient = lax.psum(gradient, "cond")
    return (state[None], wall_gradient)


def solution(mesh):
    in_specs = (
        P("cond", "slab", None, None),
        P("cond", "slab", None, None),
        P("cond", "slab", None),
        P("cond", "slab", None),
        P("cond", "slab"),
        P("cond"),
        P(),
        P(None, "slab", None),
    )
    out_specs = (P("cond", "slab", None, None), P(None, "slab", None))
    return jax.shard_map(
        on_device, mesh=mesh, in_specs=in_specs, out_specs=out_specs, check_vma=False
    )
```

profile of v0, /device:TPU:512, one launch (start us, length us, event | category | flops | bytes accessed | tf_op | source)
XLA Modules:
  0.0 481.2 jit_solution(3154809602494482971)
XLA Ops:
  0.6 0.0 copy-start.7
  0.6 0.0 copy-start.8
  0.7 0.0 copy-start.9
  0.7 0.0 copy-start.4
  0.7 0.0 copy-start.2
  0.7 2.1 slice_bitcast_fusion
  2.8 7.5 %collective-permute-start = (f32[2,512,128]{2,1,0:T(8,128)}, f32[2,512,128]{2,1,0:T(8,128)S(1)}, u32[]{:S(2)}, u32[]{:S(2)}) collective-permute-start(f32[2,512,128]{2,1,0:T(8,128)} %get-tuple-element.15), channel_id=1, source_target_pairs={{1,0},{2,1},{3,2},{4,3},{5,4},{6,5},{7,6},{8,7},{9,8},{10,9},{11,1... | collective-permute-start | bytes 1572872 | tf_op jit(solution)/shard_map/ppermute | solution.py:22
  10.3 1.9 collective-permute-start.1
  12.2 0.5 subtract_multiply_fusion
  12.7 0.5 and_convert_fusion
  13.9 1.4 dynamic-slice
  16.0 0.0 copy-done.7
  16.0 0.1 bitcast_dynamic-update-slice_fusion
  16.1 0.0 copy-done.8
  16.1 0.1 bitcast_dynamic-update-slice_fusion.1
  16.2 242.2 %all-reduce.12 = (s32[1536]{0:T(1024)S(1)}, s32[1536]{0:T(1024)S(1)}) all-reduce(s32[1536]{0:T(1024)S(1)} %bitcast_dynamic-update-slice_fusion, s32[1536]{0:T(1024)S(1)} %bitcast_dynamic-update-slice_fusion.1), channel_id=1, replica_groups=mesh['cond'=16,'slab'=48] {'slab'}, use_global_device_ids=true, to_apply=%add.11 | all-reduce | flops 3072 | bytes 24576
  258.4 0.6 fusion.42
  259.0 0.0 copy-done.9
  259.0 0.7 fusion.43
  260.3 0.0 copy-done.4
  260.4 119.6 %all_gather.11 = bf16[1,1536,128]{2,1,0:T(8,128)(2,1)S(1)} all-gather(bf16[1,32,128]{2,1,0:T(8,128)(2,1)S(1)} %copy-done.4), channel_id=1, replica_groups=mesh['cond'=16,'slab'=48] {'slab'}, dimensions={1}, use_global_device_ids=true | all-gather | bytes 401408 | tf_op jit(solution)/shard_map/all_gather | solution.py:103
  379.9 0.1 convert_bitcast_fusion
  380.0 0.0 collective-permute-done
  380.0 0.0 collective-permute-done.1
  380.0 0.1 pad_maximum_fusion.2
  380.1 0.9 fusion.3
  381.1 0.0 copy-start.6
  381.1 0.1 slice.174
  381.2 0.5 copy-done.5
  381.7 0.1 copy-done.6
  381.7 1.2 fusion.20
  382.9 0.1 fusion.45
  383.0 5.1 %collective-permute-start.2 = (f32[2,512,128]{2,1,0:T(8,128)S(1)}, f32[2,512,128]{2,1,0:T(8,128)S(1)}, u32[]{:S(2)}, u32[]{:S(2)}) collective-permute-start(f32[2,512,128]{2,1,0:T(8,128)S(1)} %get-tuple-element.13), channel_id=1, source_target_pairs={{1,0},{2,1},{3,2},{4,3},{5,4},{6,5},{7,6},{8,7},{9,8},{10,9},{11,1... | collective-permute-start | bytes 1572872 | tf_op jit(solution)/shard_map/ppermute | solution.py:22
  388.1 1.9 collective-permute-start.3
  390.1 0.1 bitcast_convert_fusion
  390.2 11.6 %collective-permute-done.2 = f32[2,512,128]{2,1,0:T(8,128)S(1)} collective-permute-done((f32[2,512,128]{2,1,0:T(8,128)S(1)}, f32[2,512,128]{2,1,0:T(8,128)S(1)}, u32[]{:S(2)}, u32[]{:S(2)}) %collective-permute-start.2) | collective-permute-done | bytes 524320 | tf_op jit(solution)/shard_map/ppermute | solution.py:22
  401.8 7.2 %collective-permute-done.3 = f32[2,512,128]{2,1,0:T(8,128)S(1)} collective-permute-done((f32[2,512,128]{2,1,0:T(8,128)S(1)}, f32[2,512,128]{2,1,0:T(8,128)S(1)}, u32[]{:S(2)}, u32[]{:S(2)}) %collective-permute-start.3) | collective-permute-done | bytes 524320 | tf_op jit(solution)/shard_map/ppermute | solution.py:20
  409.0 0.1 pad_maximum_fusion
  409.1 0.9 fusion.7
  410.0 0.1 slice.179
  410.1 1.2 fusion.27
  411.3 0.0 copy-start.3
  411.3 2.0 fusion.29
  413.3 0.0 copy-done.3
  413.4 52.9 %psum.7 = f32[2,4,512]{2,1,0:T(4,128)} all-reduce(f32[2,4,512]{2,1,0:T(4,128)S(1)} %fusion.40), channel_id=1, replica_groups=mesh['cond'=16,'slab'=48] {'cond'}, use_global_device_ids=true, to_apply=%region_2.3 | all-reduce | flops 4096 | bytes 32768 | tf_op jit(solution)/shard_map/psum | solution.py:109
  466.3 13.9 %scatter_custom_fusion = f32[2048,128]{1,0:T(8,128)S(1)} fusion(f32[2048,128]{1,0:T(8,128)S(1)} %bitcast.36, s32[1536]{0:T(1024)} %get-tuple-element.9, bf16[1,1536,128]{2,1,0:T(8,128)(2,1)S(1)} %all_gather.11, f32[2048,128]{1,0:T(8,128)S(1)} %bitcast_convert_fusion, s32[2048]{0:T(1024)S(1)} %pad_clamp_fusion), kind=kCustom, calls=%fused_computation.64 | custom fusion | flops 589824 | bytes 2498560 | tf_op jit(solution)/shard_map/scatter-add | solution.py:80
  480.2 0.0 copy-start.1
  480.2 1.0 copy-done.1
  (10 shorter events, 0.0 us)
Async XLA Ops:
  0.6 15.4 %copy-start.7 = (s32[1,32]{1,0:T(1,128)S(1)}, s32[1,32]{1,0:T(1,128)}, u32[]{:S(2)}) copy-start(s32[1,32]{1,0:T(1,128)} %param.12) | copy-start | bytes 388
  0.6 15.5 %copy-start.8 = (s32[1,32,1]{1,2,0:T(1,128)S(1)}, s32[1,32,1]{1,2,0:T(1,128)}, u32[]{:S(2)}) copy-start(s32[1,32,1]{1,2,0:T(1,128)} %param.11) | copy-start | bytes 388
  0.7 258.4 %copy-start.9 = (f32[8]{0:T(128)S(1)}, f32[8]{0:T(128)}, u32[]{:S(2)}) copy-start(f32[8]{0:T(128)} %param.14) | copy-start | bytes 100
  0.7 259.7 %copy-start.4 = (bf16[1,32,128]{2,1,0:T(8,128)(2,1)S(1)}, bf16[1,32,128]{2,1,0:T(8,128)(2,1)}, u32[]{:S(2)}) copy-start(bf16[1,32,128]{2,1,0:T(8,128)(2,1)} %param.10) | copy-start | bytes 24580
  0.7 379.2 %copy-start.2 = (bf16[1,4,512,128]{3,2,1,0:T(8,128)(2,1)S(1)}, bf16[1,4,512,128]{3,2,1,0:T(8,128)(2,1)}, u32[]{:S(2)}) copy-start(bf16[1,4,512,128]{3,2,1,0:T(8,128)(2,1)} %param.9) | copy-start | bytes 1572868
  2.8 377.2 %copy-start = (f32[1,4,512,128]{3,2,1,0:T(8,128)S(1)}, f32[1,4,512,128]{3,2,1,0:T(8,128)}, u32[]{:S(2)}) copy-start(f32[1,4,512,128]{3,2,1,0:T(8,128)} %param.8) | copy-start | bytes 3145732
  2.8 377.2 %collective-permute-start = (f32[2,512,128]{2,1,0:T(8,128)}, f32[2,512,128]{2,1,0:T(8,128)S(1)}, u32[]{:S(2)}, u32[]{:S(2)}) collective-permute-start(f32[2,512,128]{2,1,0:T(8,128)} %get-tuple-element.15), channel_id=1, source_target_pairs={{1,0},{2,1},{3,2},{4,3},{5,4},{6,5},{7,6},{8,7},{9,8},{10,9},{11,1... | collective-permute-start | bytes 1572872 | tf_op jit(solution)/shard_map/ppermute | solution.py:22
  10.3 369.7 %collective-permute-start.1 = (f32[2,512,128]{2,1,0:T(8,128)S(1)}, f32[2,512,128]{2,1,0:T(8,128)S(1)}, u32[]{:S(2)}, u32[]{:S(2)}) collective-permute-start(f32[2,512,128]{2,1,0:T(8,128)S(1)} %get-tuple-element.14), channel_id=1, source_target_pairs={{0,1},{1,2},{2,3},{3,4},{4,5},{5,6},{6,7},{7,8},{8,9},{9,10},{10,1... | collective-permute-start | bytes 1572872 | tf_op jit(solution)/shard_map/ppermute | solution.py:20
  381.1 0.6 copy-start.5
  381.1 0.7 copy-start.6
  383.0 18.8 %collective-permute-start.2 = (f32[2,512,128]{2,1,0:T(8,128)S(1)}, f32[2,512,128]{2,1,0:T(8,128)S(1)}, u32[]{:S(2)}, u32[]{:S(2)}) collective-permute-start(f32[2,512,128]{2,1,0:T(8,128)S(1)} %get-tuple-element.13), channel_id=1, source_target_pairs={{1,0},{2,1},{3,2},{4,3},{5,4},{6,5},{7,6},{8,7},{9,8},{10,9},{11,1... | collective-permute-start | bytes 1572872 | tf_op jit(solution)/shard_map/ppermute | solution.py:22
  388.1 20.9 %collective-permute-start.3 = (f32[2,512,128]{2,1,0:T(8,128)S(1)}, f32[2,512,128]{2,1,0:T(8,128)S(1)}, u32[]{:S(2)}, u32[]{:S(2)}) collective-permute-start(f32[2,512,128]{2,1,0:T(8,128)S(1)} %get-tuple-element.12), channel_id=1, source_target_pairs={{0,1},{1,2},{2,3},{3,4},{4,5},{5,6},{6,7},{7,8},{8,9},{9,10},{10,1... | collective-permute-start | bytes 1572872 | tf_op jit(solution)/shard_map/ppermute | solution.py:20
  411.3 2.1 copy-start.3
  480.2 1.0 copy-start.1
where the time goes:
time: 482 us; the launch traced here: 481 us
  blocking collectives  415 us (86%)
  other arithmetic  22.9 us (5%)
  waiting for transfers between devices  18.8 us (4%)
  starting transfers between devices  16.4 us (3%)
  local copies, waits for them, and re-layouts  5.49 us (1%)
    unnamed x1, blocking collectives  242 us
    all_gather x1, blocking collectives, on_device(): lax.all_gather(targets, 'slab', axis=1, tiled=True)  120 us
    psum x1, blocking collectives, on_device(): wall_gradient = lax.psum(gradient, 'cond')  52.9 us
    scatter-add x1, other arithmetic, inject(): return shaped.at[row_index].add(source, mode='drop').reshape(state.shape)  13.9 us
    ppermute x2, starting transfers between devices, extended_2(): lax.ppermute(head, axis, [((i + 1) % count, i) for i in range(ends)])  12.6 us
    ppermute x2, waiting for transfers between devices, extended_2(): lax.ppermute(head, axis, [((i + 1) % count, i) for i in range(ends)])  11.6 us
  transfers between devices with their start and end apart: 4, of which 2 were waited for; matrix products, arithmetic and copies ran while one was open for 1% of the time, Pallas kernels for 0%

commit v1 on v0

v1 whole, which is shorter than its diff:
```python
import functools

import jax
import jax.numpy as jnp
from jax import lax
from jax.experimental import pallas as pl
from jax.experimental.pallas import tpu as pltpu
from jax.sharding import PartitionSpec as P

MESH = pl.DeviceIdType.MESH
F32 = jnp.float32
BF16 = jnp.bfloat16

mobility_step = 0.02
stiffness_step = 0.01
transport_step = 0.125
wall_weight = 0.25

CHUNKS = 4
PAD = 8


def kernel(
    n_cond, n_slab, adj, ph, tgt, own, cell, ridx, rates, mask, out, grad,
    S, PB, F, S1, OB, H, LO, SB, RB, tv, ov, cv, mv, ST, RT, TA, G, GS, RR, FIN, tot,
    in_sem, ss, rs, ts, tr, gs, gr, fs, fr, out_sem, go, go2,
):
    ny = S.shape[1] - 2 * PAD
    nz = S.shape[2]
    nx = S.shape[0]
    c = lax.axis_index("cond")
    me = lax.axis_index("slab")
    last = n_slab - 1
    has = (me > 0, me < last)
    peer = (me - 1, me + 1)
    near = (0, nx - 1)
    far = (1, nx - 2)
    step = ny // CHUNKS

    loads = [pltpu.make_async_copy(adj.at[0, j], S.at[j, pl.ds(PAD, ny)], in_sem.at[j]) for j in range(nx)]
    ph_load = pltpu.make_async_copy(ph.at[0], PB, in_sem.at[nx])
    small = [
        pltpu.make_async_copy(tgt.at[0], tv, in_sem.at[nx + 1]),
        pltpu.make_async_copy(own, ov, in_sem.at[nx + 2]),
        pltpu.make_async_copy(cell, cv, in_sem.at[nx + 3]),
        pltpu.make_async_copy(mask, mv, in_sem.at[nx + 4]),
    ]
    for j in (0, nx - 1, 1, nx - 2):
        loads[j].start()
    for cp in small:
        cp.start()
    ph_load.start()

    bar = pltpu.get_barrier_semaphore()
    for s in range(2):
        @pl.when(has[s])
        def _():
            pl.semaphore_signal(bar, inc=1, device_id=(c, peer[s]), device_id_type=MESH)

    @pl.when(me < last - 1)
    def _():
        pl.semaphore_signal(bar, inc=1, device_id=(c, last), device_id_type=MESH)

    @pl.when(c > 0)
    def _():
        pl.semaphore_signal(bar, inc=1, device_id=(0, me), device_id_type=MESH)

    lane = lax.broadcasted_iota(jnp.int32, (1, nz), 1)
    keep_lo = (lane > 0).astype(F32)
    keep_hi = (lane < nz - 1).astype(F32)
    height = (lane.astype(F32) + 0.5) / nz
    profile = 4.0 * height * (1.0 - height)
    inflow = F32(0.0)
    for i in range(rates.shape[0]):
        inflow = inflow + jnp.where(ridx[0] == i, rates[i], 0.0)
    drift = (transport_step * inflow) * profile

    def in_plane(ref, j, r, n):
        x = ref[j, pl.ds(r + PAD, n), :]
        zsum = pltpu.roll(x, 1, 1) * keep_lo + pltpu.roll(x, nz - 1, 1) * keep_hi
        return zsum + ref[j, pl.ds(r + (PAD - 1), n), :] + ref[j, pl.ds(r + (PAD + 1), n), :] - 6.0 * x

    def rows(lo, hi, n, body):
        def run(i, _):
            body(pl.multiple_of(lo + i * n, 16))
            return 0
        lax.fori_loop(0, (hi - lo) // n, run, 0)

    def mobility(j, r, n):
        p = PB[j, pl.ds(r, n), :].astype(F32)
        return (3.0 * mobility_step) * (p * p) - mobility_step

    zpad = jnp.zeros((PAD, nz), F32)
    for ref in (S, F, S1):
        for j in range(nx):
            ref[j, pl.ds(0, PAD), :] = zpad
            ref[j, pl.ds(PAD + ny, PAD), :] = zpad
    for ref in (H, LO):
        for j in range(2):
            ref[j, pl.ds(0, PAD), :] = zpad
            ref[j, pl.ds(PAD + ny, PAD), :] = zpad

    def split(ref, phase, s, lo, hi):
        def body(r):
            x = ref[near[s], pl.ds(r + PAD, 16), :]
            h = x.astype(BF16)
            SB[phase, s, 0, pl.ds(r, 16), :] = h
            LO[s, pl.ds(r + PAD, 16), :] = x - h.astype(F32)
        rows(lo, hi, 16, body)

    def residue(ref, phase, s, lo, hi):
        def body(r):
            q = -2.0 * stiffness_step * in_plane(LO, s, r, 16) - stiffness_step * ref[far[s], pl.ds(r + PAD, 16), :]
            SB[phase, s, 1, pl.ds(r, 16), :] = q.astype(BF16)
        rows(lo, hi, 16, body)

    def piece(phase, s, k, lo, hi, p):
        return pltpu.make_async_remote_copy(
            src_ref=SB.at[phase, s, p, pl.ds(lo, hi - lo)],
            dst_ref=RB.at[phase, 1 - s, p, pl.ds(lo, hi - lo)],
            send_sem=ss.at[phase, s, p, k],
            recv_sem=rs.at[phase, 1 - s, p, k],
            device_id=(c, peer[s]),
            device_id_type=MESH,
        )

    def landing(phase, s, k, lo, hi, p):
        return pltpu.make_async_remote_copy(
            src_ref=SB.at[phase, 1 - s, p, pl.ds(lo, hi - lo)],
            dst_ref=RB.at[phase, s, p, pl.ds(lo, hi - lo)],
            send_sem=ss.at[phase, 1 - s, p, k],
            recv_sem=rs.at[phase, s, p, k],
            device_id=(c, peer[s]),
            device_id_type=MESH,
        )

    cuts = [[(k * step, (k + 1) * step) for k in range(CHUNKS)]]
    for lag in (32,):
        edges = [0] + [k * step - lag for k in range(1, CHUNKS)] + [ny]
        cuts.append(list(zip(edges[:-1], edges[1:])))

    def lagged(phase, k, lag):
        lo = 0 if k == 0 else cuts[phase][k][0] - lag
        hi = ny if k == CHUNKS - 1 else cuts[phase][k][1] - lag
        return lo, hi

    for s in range(2):
        loads[near[s]].wait()
        split(S, 0, s, 0, ny)
        loads[far[s]].wait()
        residue(S, 0, s, 0, ny)

    greeted = has[0].astype(jnp.int32) + has[1].astype(jnp.int32)
    greeted = greeted + jnp.where(me == last, last - 1, 0) + jnp.where(c == 0, n_cond - 1, 0)
    pl.semaphore_wait(bar, greeted)
    for k in range(CHUNKS):
        for s in range(2):
            @pl.when(has[s])
            def _():
                for p in range(2):
                    piece(0, s, k, *cuts[0][k], p).start()

    @pl.when(me == last)
    def _():
        def tell(d, _):
            pl.semaphore_signal(go, inc=1, device_id=(c, d), device_id_type=MESH)
            return 0
        lax.fori_loop(0, last, tell, 0)

    @pl.when(c == 0)
    def _():
        def tell(d, _):
            pl.semaphore_signal(go2, inc=1, device_id=(d, me), device_id_type=MESH)
            return 0
        lax.fori_loop(1, n_cond, tell, 0)

    for cp in small:
        cp.wait()
    n_rows = tv.shape[0]
    match = (ov[...] == lax.broadcasted_iota(jnp.int32, (n_slab, n_rows), 0)).astype(F32)
    upper = (
        lax.broadcasted_iota(jnp.int32, (n_rows, n_rows), 0) < lax.broadcasted_iota(jnp.int32, (n_rows, n_rows), 1)
    ).astype(BF16)
    earlier = jnp.dot(match.astype(BF16), upper, preferred_element_type=F32)
    first = jnp.where(earlier < 0.5, match, 0.0)
    second = match - first
    code = cv[...].astype(F32) + 16.0
    lanes = lax.broadcasted_iota(jnp.int32, (n_slab, nz), 1)
    high = jnp.zeros((n_slab, nz), F32)
    low = jnp.zeros((n_slab, nz), F32)
    for i, pick in enumerate((first, second)):
        ST[:, i, :] = jnp.dot(pick.astype(BF16), tv[...], preferred_element_type=F32).astype(ST.dtype)
        mine = jnp.sum(pick * code, axis=1, keepdims=True)
        hi_part = jnp.floor(mine * (1.0 / 16.0))
        here = lanes == me + i * n_slab
        high = jnp.where(here, hi_part, high)
        low = jnp.where(here, mine - 16.0 * hi_part, low)
    ST[:, 2, :] = high.astype(ST.dtype)
    ST[:, 3, :] = low.astype(ST.dtype)
    RT[me] = ST[me]

    def row_copy(d, slot):
        return pltpu.make_async_remote_copy(
            src_ref=ST.at[d], dst_ref=RT.at[slot], send_sem=ts.at[d], recv_sem=tr.at[slot],
            device_id=(c, d), device_id_type=MESH,
        )

    def send_rows():
        @pl.when(me < last)
        def _():
            pl.semaphore_wait(go, 1)

        def one(i, _):
            row_copy(lax.rem(me + i, n_slab), me).start()
            return 0
        lax.fori_loop(1, n_slab, one, 0)

    late = me >= n_slab - n_slab // 6
    middle = jnp.logical_and(me >= n_slab // 2, jnp.logical_not(late))

    @pl.when(late)
    def _():
        send_rows()

    ghost = (has[0].astype(F32), has[1].astype(F32))

    def local_step(src, dst, padded):
        def laps(r):
            for j in range(nx):
                v = in_plane(src, j, r, 16)
                for o in (j - 1, j + 1):
                    if 0 <= o < nx:
                        v = v + src[o, pl.ds(r + PAD, 16), :]
                F[j, pl.ds(r + PAD, 16), :] = v
        rows(0, ny, 16, laps)

        def update(r):
            for j in range(nx):
                lap2 = in_plane(F, j, r, 16)
                for o in (j - 1, j + 1):
                    if 0 <= o < nx:
                        lap2 = lap2 + F[o, pl.ds(r + PAD, 16), :]
                x = src[j, pl.ds(r + PAD, 16), :]
                for s in range(2):
                    if j == near[s]:
                        lap2 = lap2 + ghost[s] * x
                moved = src[j, pl.ds(r + (PAD + 1), 16), :] - src[j, pl.ds(r + (PAD - 1), 16), :]
                v = x + mobility(j, r, 16) * F[j, pl.ds(r + PAD, 16), :] - stiffness_step * lap2 + drift * moved
                dst[j, pl.ds(r + padded, 16), :] = v
        rows(0, ny, 16, update)

    def unpack(phase, s, lo, hi):
        def body(r):
            H[s, pl.ds(r + PAD, 16), :] = RB[phase, s, 0, pl.ds(r, 16), :].astype(F32)
        rows(lo, hi, 16, body)

    def correct(phase, dst, padded, s, lo, hi):
        def body(r):
            h = H[s, pl.ds(r + PAD, 16), :]
            v = dst[near[s], pl.ds(r + padded, 16), :] + mobility(near[s], r, 16) * h
            v = v - 2.0 * stiffness_step * in_plane(H, s, r, 16) + RB[phase, s, 1, pl.ds(r, 16), :].astype(F32)
            dst[near[s], pl.ds(r + padded, 16), :] = v
            dst[far[s], pl.ds(r + padded, 16), :] = dst[far[s], pl.ds(r + padded, 16), :] - stiffness_step * h
        rows(lo, hi, 16, body)

    ph_load.wait()
    local_step(S, S1, PAD)
    for k in range(CHUNKS):
        for s in range(2):
            @pl.when(has[s])
            def _():
                for p in range(2):
                    landing(0, s, k, *cuts[0][k], p).wait_recv()
                unpack(0, s, *cuts[0][k])
                lo, hi = lagged(0, k, 16)
                correct(0, S1, PAD, s, lo, hi)
                split(S1, 1, s, lo, hi)
                residue(S1, 1, s, *cuts[1][k])
                for p in range(2):
                    piece(1, s, k, *cuts[1][k], p).start()
        if k == 1:
            @pl.when(middle)
            def _():
                send_rows()

    @pl.when(me < n_slab // 2)
    def _():
        send_rows()

    local_step(S1, OB, 0)

    def walls(lo, hi):
        for b in range(lo // nz, hi // nz):
            total = jnp.zeros((2 * nx, nz), F32)
            for j in range(nx):
                p = PB[j, pl.ds(b * nz, nz), :].astype(F32)
                x = (1.0 - p * p) * (S1[j, pl.ds(b * nz + PAD, nz), :] + OB[j, pl.ds(b * nz, nz), :])
                row = lax.broadcasted_iota(jnp.int32, (2 * nx, nz), 0)
                col = lax.broadcasted_iota(jnp.int32, (2 * nx, nz), 1)
                pick = jnp.logical_or(
                    jnp.logical_and(row == j, col == 0), jnp.logical_and(row == nx + j, col == nz - 1)
                ).astype(F32)
                total = total + lax.dot_general(
                    pick, x, (((1,), (1,)), ((), ())), precision=lax.Precision.HIGHEST, preferred_element_type=F32
                )
            G[:, pl.ds(b * nz, nz)] = total

    done = 0
    for k in range(CHUNKS):
        lo, hi = lagged(1, k, 16)
        for s in range(2):
            @pl.when(has[s])
            def _():
                for p in range(2):
                    landing(1, s, k, *cuts[1][k], p).wait_recv()
                unpack(1, s, *cuts[1][k])
                correct(1, OB, 0, s, lo, hi)
        ready = hi // nz * nz
        walls(done, ready)
        done = ready

    n_red = GS.shape[0]
    stride = n_cond // n_red
    for r in range(n_red):
        GS[r] = G[r : r + 1, :]

    @pl.when(c > 0)
    def _():
        pl.semaphore_wait(go2, 1)

    def part(r, slot):
        return pltpu.make_async_remote_copy(
            src_ref=GS.at[r], dst_ref=RR.at[slot], send_sem=gs.at[r], recv_sem=gr.at[slot],
            device_id=(r * stride, me), device_id_type=MESH,
        )

    def whole(d, r):
        return pltpu.make_async_remote_copy(
            src_ref=tot, dst_ref=FIN.at[r], send_sem=fs.at[d], recv_sem=fr.at[r],
            device_id=(d, me), device_id_type=MESH,
        )

    for r in range(n_red):
        @pl.when(c != r * stride)
        def _():
            part(r, c).start()

    mine_r = c // stride
    reducer = lax.rem(c, stride) == 0

    def rows_in(i, _):
        d = lax.rem(me + i, n_slab)
        row_copy(d, d).wait_recv()
        return 0
    lax.fori_loop(1, n_slab, rows_in, 0)
    TA[...] = jnp.zeros_like(TA)
    for i in range(2):
        TA[pl.ds(i * n_slab, n_slab), pl.ds(0, nz)] = RT[:, i, :].astype(BF16)
    TA[:, pl.ds(nz, nz)] = jnp.ones((nz, nz), BF16)
    hi_sum = jnp.sum(RT[:, 2, :].astype(F32), axis=0, keepdims=True)
    lo_sum = jnp.sum(RT[:, 3, :].astype(F32), axis=0, keepdims=True)
    where_to = ((hi_sum - 1.0) * 16.0 + lo_sum).astype(jnp.int32)
    per = ny // nz
    for j in range(nx):
        def inject(b, _):
            r = pl.multiple_of(b * nz, nz)
            at = lax.broadcasted_iota(jnp.int32, (nz, nz), 0) + (j * ny + r)
            hit = (at == where_to).astype(F32).astype(BF16)
            both = jnp.dot(hit, TA[...], preferred_element_type=F32)
            p = PB[j, pl.ds(r, nz), :].astype(F32)
            OB[j, pl.ds(r, nz), :] = OB[j, pl.ds(r, nz), :] + (p * both[:, nz:] - both[:, :nz])
            return 0
        lax.fori_loop(0, per, inject, 0)
        pltpu.make_async_copy(OB.at[j], out.at[0, j], out_sem.at[j]).start()

    @pl.when(reducer)
    def _():
        tot[...] = GS[mine_r]

        def add(i, _):
            d = lax.rem(c + i, n_cond)
            part(mine_r, d).wait_recv()
            tot[...] = tot[...] + RR[d]
            return 0
        lax.fori_loop(1, n_cond, add, 0)

        def tell(i, _):
            whole(lax.rem(c + i, n_cond), mine_r).start()
            return 0
        lax.fori_loop(1, n_cond, tell, 0)
        FIN[mine_r] = tot[...]

    for r in range(n_red):
        @pl.when(c != r * stride)
        def _():
            whole(c, r).wait_recv()
    for w in range(2):
        for x in range(nx):
            grad[w, x : x + 1, :] = (wall_weight * mv[w, x : x + 1, :].astype(F32)) * FIN[w * nx + x]

    for phase in range(2):
        for s in range(2):
            @pl.when(has[s])
            def _():
                for k in range(CHUNKS):
                    for p in range(2):
                        piece(phase, s, k, *cuts[phase][k], p).wait_send()

    def rows_out(i, _):
        d = lax.rem(me + i, n_slab)
        row_copy(d, me).wait_send()
        return 0
    lax.fori_loop(1, n_slab, rows_out, 0)
    for r in range(n_red):
        @pl.when(c != r * stride)
        def _():
            part(r, c).wait_send()

    @pl.when(reducer)
    def _():
        def sent(i, _):
            whole(lax.rem(c + i, n_cond), mine_r).wait_send()
            return 0
        lax.fori_loop(1, n_cond, sent, 0)
    for j in range(nx):
        pltpu.make_async_copy(OB.at[j], out.at[0, j], out_sem.at[j]).wait()


def on_device(adjoint, phase, targets, owners, target_cell, rate_index, inflow_rates, wall_mask):
    n_cond = lax.axis_size("cond")
    n_slab = lax.axis_size("slab")
    _, nx, ny, nz = adjoint.shape
    n_rows = targets.shape[1]
    n_red = 2 * nx
    any_space = pl.BlockSpec(memory_space=pl.ANY)
    smem = pl.BlockSpec(memory_space=pltpu.SMEM)
    dma = pltpu.SemaphoreType.DMA
    padded = ny + 2 * PAD
    call = pl.pallas_call(
        functools.partial(kernel, n_cond, n_slab),
        out_shape=(
            jax.ShapeDtypeStruct(adjoint.shape, F32),
            jax.ShapeDtypeStruct(wall_mask.shape, F32),
        ),
        in_specs=[any_space] * 5 + [smem, smem, any_space],
        out_specs=(any_space, pl.BlockSpec(memory_space=pltpu.VMEM)),
        scratch_shapes=[
            pltpu.VMEM((nx, padded, nz), F32),
            pltpu.VMEM((nx, ny, nz), BF16),
            pltpu.VMEM((nx, padded, nz), F32),
            pltpu.VMEM((nx, padded, nz), F32),
            pltpu.VMEM((nx, ny, nz), F32),
            pltpu.VMEM((2, padded, nz), F32),
            pltpu.VMEM((2, padded, nz), F32),
            pltpu.VMEM((2, 2, 2, ny, nz), BF16),
            pltpu.VMEM((2, 2, 2, ny, nz), BF16),
            pltpu.VMEM((n_rows, nz), BF16),
            pltpu.VMEM((1, n_rows), jnp.int32),
            pltpu.VMEM((1, n_rows), jnp.int32),
            pltpu.VMEM(wall_mask.shape, jnp.int32),
            pltpu.VMEM((n_slab, 4, nz), ROW),
            pltpu.VMEM((n_slab, 4, nz), ROW),
            pltpu.VMEM((nz, 2 * nz), BF16),
            pltpu.VMEM((n_red, ny), F32),
            pltpu.VMEM((n_red, 1, ny), F32),
            pltpu.VMEM((n_cond, 1, ny), F32),
            pltpu.VMEM((n_red, 1, ny), F32),
            pltpu.VMEM((1, ny), F32),
            dma((nx + 5,)),
            dma((2, 2, 2, CHUNKS)),
            dma((2, 2, 2, CHUNKS)),
            dma((n_slab,)),
            dma((n_slab,)),
            dma((n_red,)),
            dma((n_cond,)),
            dma((n_cond,)),
            dma((n_red,)),
            dma((nx,)),
            pltpu.SemaphoreType.REGULAR,
            pltpu.SemaphoreType.REGULAR,
        ],
        compiler_params=pltpu.CompilerParams(
            collective_id=0, has_side_effects=True, vmem_limit_bytes=40 * 1024 * 1024
        ),
    )
    owner_row = owners.reshape(1, n_rows)
    return call(adjoint, phase, targets, owner_row, target_cell, rate_index, inflow_rates, wall_mask)


ROW = F32


def solution(mesh):
    in_specs = (
        P("cond", "slab", None, None),
        P("cond", "slab", None, None),
        P("cond", "slab", None),
        P("cond", "slab", None),
        P("cond", "slab"),
        P("cond"),
        P(),
        P(None, "slab", None),
    )
    out_specs = (P("cond", "slab", None, None), P(None, "slab", None))
    return jax.shard_map(
        on_device, mesh=mesh, in_specs=in_specs, out_specs=out_specs, check_vma=False
    )
```

time: 482 us -> 70.4 us (0.15)
  the two profiles are of different devices: /device:TPU:512 before, /device:TPU:569 now
where the time goes in v1:
time: 70.4 us; the launch traced here: 70.1 us
  Pallas kernels  62.9 us (89%)
  local copies, waits for them, and re-layouts  5.92 us (8%)
  between operations  1.32 us (2%)
    pallas_call x1, Pallas kernels, on_device(): call(adjoint, phase, targets, owner_row, target_cell, rate_index, inflow_...  62.9 us
    unnamed x16, local copies, waits for them, and re-layouts  5.92 us

profile of v1, /device:TPU:569, one launch (start us, length us, event | category | flops | bytes accessed | tf_op | source)
XLA Modules:
  0.0 70.1 jit_solution(11293844232235350593)
XLA Ops:
  1.3 0.0 copy-start.4
  1.3 0.0 copy-start.5
  1.3 0.0 copy-start.6
  1.3 0.6 copy-done.4
  1.9 0.0 copy-done.5
  1.9 0.0 copy-done.6
  2.0 0.0 copy-start
  2.0 1.2 %copy-done = f32[1,4,512,128]{3,2,1,0:T(8,128)S(1)} copy-done((f32[1,4,512,128]{3,2,1,0:T(8,128)S(1)}, f32[1,4,512,128]{3,2,1,0:T(8,128)}, u32[]{:S(2)}) %copy-start) | copy-done | bytes 1048600
  3.2 0.0 copy-start.1
  3.2 1.0 %copy-done.1 = bf16[1,4,512,128]{3,2,1,0:T(8,128)(2,1)S(1)} copy-done((bf16[1,4,512,128]{3,2,1,0:T(8,128)(2,1)S(1)}, bf16[1,4,512,128]{3,2,1,0:T(8,128)(2,1)}, u32[]{:S(2)}) %copy-start.1) | copy-done | bytes 524312
  4.2 0.0 copy-start.2
  4.2 0.7 %copy-done.2 = s32[2,4,512]{2,1,0:T(4,128)S(1)} copy-done((s32[2,4,512]{2,1,0:T(4,128)S(1)}, s32[2,4,512]{2,1,0:T(4,128)}, u32[]{:S(2)}) %copy-start.2) | copy-done | bytes 16408
  5.0 0.0 copy-start.3
  5.0 0.7 copy-done.3
  5.6 62.9 %shard_map.95 = (f32[1,4,512,128]{3,2,1,0:T(8,128)S(1)}, f32[2,4,512]{2,1,0:T(4,128)S(1)}) custom-call(f32[1,4,512,128]{3,2,1,0:T(8,128)S(1)} %copy-done, bf16[1,4,512,128]{3,2,1,0:T(8,128)(2,1)S(1)} %copy-done.1, bf16[1,32,128]{2,1,0:T(8,128)(2,1)S(1)} %copy-done.3, s32[1,32]{1,0:T(1,128)S(1)} %bitcast.1, s32[1,32]{1,0:T(1,128)S(1)} %copy-done.5, ...), custom_call_target="tpu_custom_call" | custom-call | tf_op jit(solution)/shard_map/pallas_call | solution.py:487
  68.5 1.0 %copy.13 = f32[1,4,512,128]{3,2,1,0:T(8,128)} copy(f32[1,4,512,128]{3,2,1,0:T(8,128)S(1)} %get-tuple-element.4) | data formatting | bytes 2097152
  69.5 0.6 copy.14
Async XLA Ops:
  1.3 0.7 copy-start.4
  1.3 0.7 copy-start.5
  1.3 0.7 copy-start.6
  2.0 1.2 %copy-start = (f32[1,4,512,128]{3,2,1,0:T(8,128)S(1)}, f32[1,4,512,128]{3,2,1,0:T(8,128)}, u32[]{:S(2)}) copy-start(f32[1,4,512,128]{3,2,1,0:T(8,128)} %adj.1) | copy-start | bytes 3145732
  3.2 1.0 %copy-start.1 = (bf16[1,4,512,128]{3,2,1,0:T(8,128)(2,1)S(1)}, bf16[1,4,512,128]{3,2,1,0:T(8,128)(2,1)}, u32[]{:S(2)}) copy-start(bf16[1,4,512,128]{3,2,1,0:T(8,128)(2,1)} %ph.1) | copy-start | bytes 1572868
  4.2 0.7 %copy-start.2 = (s32[2,4,512]{2,1,0:T(4,128)S(1)}, s32[2,4,512]{2,1,0:T(4,128)}, u32[]{:S(2)}) copy-start(s32[2,4,512]{2,1,0:T(4,128)} %mask.1) | copy-start | bytes 49156
  5.0 0.7 copy-start.3

commit v2 on v1

v2 whole, which is shorter than its diff:
```python
import functools

import jax
import jax.numpy as jnp
from jax import lax
from jax.experimental import pallas as pl
from jax.experimental.pallas import tpu as pltpu
from jax.sharding import PartitionSpec as P

MESH = pl.DeviceIdType.MESH
F32 = jnp.float32
BF16 = jnp.bfloat16

mobility_step = 0.02
stiffness_step = 0.01
transport_step = 0.125
wall_weight = 0.25

CHUNKS = 4
HELD = 2
PAD = 8


def kernel(
    n_cond, n_slab, adj, ph, tgt, own, cell, ridx, rates, mask, out, grad,
    S, PB, F, S1, H, LO, SB, RB, tv, ov, cv, mv, fv, ST, RT, TA, BW, EP, WS, WR, GS, RR, FIN, tot,
    in_sem, ss, rs, ts, tr, gs, gr, fs, fr, ws, wr, go, go2, up,
):
    OB = out.at[0]
    ny = S.shape[1] - 2 * PAD
    nz = S.shape[2]
    nx = S.shape[0]
    c = lax.axis_index("cond")
    me = lax.axis_index("slab")
    last = n_slab - 1
    has = (me > 0, me < last)
    peer = (me - 1, me + 1)
    near = (0, nx - 1)
    far = (1, nx - 2)
    step = ny // CHUNKS

    loads = [pltpu.make_async_copy(adj.at[0, j], S.at[j, pl.ds(PAD, ny)], in_sem.at[j]) for j in range(nx)]
    ph_load = pltpu.make_async_copy(ph.at[0], PB, in_sem.at[nx])
    small = [
        pltpu.make_async_copy(tgt.at[0], tv, in_sem.at[nx + 1]),
        pltpu.make_async_copy(own, ov, in_sem.at[nx + 2]),
        pltpu.make_async_copy(cell, cv, in_sem.at[nx + 3]),
        pltpu.make_async_copy(mask, mv, in_sem.at[nx + 4]),
        pltpu.make_async_copy(rates, fv, in_sem.at[nx + 5]),
    ]
    for j in (0, nx - 1, 1, nx - 2):
        loads[j].start()
    for cp in small:
        cp.start()
    ph_load.start()

    bar = pltpu.get_barrier_semaphore()
    for s in range(2):
        @pl.when(has[s])
        def _():
            pl.semaphore_signal(bar, inc=1, device_id=(c, peer[s]), device_id_type=MESH)

    half = n_slab // 2
    upper = me >= half
    hub = jnp.where(upper, last, half - 1)

    @pl.when(me < hub - 1)
    def _():
        pl.semaphore_signal(bar, inc=1, device_id=(c, hub), device_id_type=MESH)

    @pl.when(c > 0)
    def _():
        pl.semaphore_signal(bar, inc=1, device_id=(0, me), device_id_type=MESH)

    @pl.when(jnp.logical_not(upper))
    def _():
        def greet(d, _):
            pl.semaphore_signal(bar, inc=1, device_id=(c, d), device_id_type=MESH)
            return 0
        lax.fori_loop(jnp.where(me == half - 1, half + 1, half), n_slab, greet, 0)

    lane = lax.broadcasted_iota(jnp.int32, (1, nz), 1)
    keep_lo = (lane > 0).astype(F32)
    keep_hi = (lane < nz - 1).astype(F32)
    height = (lane.astype(F32) + 0.5) / nz
    profile = 4.0 * height * (1.0 - height)

    def in_plane(ref, j, r, n):
        x = ref[j, pl.ds(r + PAD, n), :]
        zsum = pltpu.roll(x, 1, 1) * keep_lo + pltpu.roll(x, nz - 1, 1) * keep_hi
        return zsum + ref[j, pl.ds(r + (PAD - 1), n), :] + ref[j, pl.ds(r + (PAD + 1), n), :] - 6.0 * x

    def rows(lo, hi, body):
        r = lo
        while r < hi:
            n = min(64, hi - r)
            body(r, n)
            r += n

    def mobility(j, r, n):
        p = PB[j, pl.ds(r, n), :].astype(F32)
        return (3.0 * mobility_step) * (p * p) - mobility_step

    zpad = jnp.zeros((PAD, nz), F32)
    for ref in (S, F, S1):
        for j in range(nx):
            ref[j, pl.ds(0, PAD), :] = zpad
            ref[j, pl.ds(PAD + ny, PAD), :] = zpad
    for ref in (H, LO):
        for j in range(2):
            ref[j, pl.ds(0, PAD), :] = zpad
            ref[j, pl.ds(PAD + ny, PAD), :] = zpad

    def split(ref, phase, s, lo, hi):
        def body(r, n):
            x = ref[near[s], pl.ds(r + PAD, n), :]
            h = x.astype(BF16)
            SB[phase, s, 0, pl.ds(r, n), :] = h
            LO[s, pl.ds(r + PAD, n), :] = x - h.astype(F32)
        rows(lo, hi, body)

    def residue(ref, phase, s, lo, hi):
        def body(r, n):
            q = -2.0 * stiffness_step * in_plane(LO, s, r, n) - stiffness_step * ref[far[s], pl.ds(r + PAD, n), :]
            SB[phase, s, 1, pl.ds(r, n), :] = q.astype(BF16)
        rows(lo, hi, body)

    def piece(phase, s, k, lo, hi):
        return pltpu.make_async_remote_copy(
            src_ref=SB.at[phase, s, :, pl.ds(lo, hi - lo)],
            dst_ref=RB.at[phase, 1 - s, :, pl.ds(lo, hi - lo)],
            send_sem=ss.at[phase, s, k],
            recv_sem=rs.at[phase, 1 - s, k],
            device_id=(c, peer[s]),
            device_id_type=MESH,
        )

    def landing(phase, s, k, lo, hi):
        return pltpu.make_async_remote_copy(
            src_ref=SB.at[phase, 1 - s, :, pl.ds(lo, hi - lo)],
            dst_ref=RB.at[phase, s, :, pl.ds(lo, hi - lo)],
            send_sem=ss.at[phase, 1 - s, k],
            recv_sem=rs.at[phase, s, k],
            device_id=(c, peer[s]),
            device_id_type=MESH,
        )

    cuts = [[(k * step, (k + 1) * step) for k in range(CHUNKS)]]
    for lag in (32,):
        edges = [0] + [k * step - lag for k in range(1, CHUNKS)] + [ny]
        cuts.append(list(zip(edges[:-1], edges[1:])))

    def lagged(phase, k, lag):
        lo = 0 if k == 0 else cuts[phase][k][0] - lag
        hi = ny if k == CHUNKS - 1 else cuts[phase][k][1] - lag
        return lo, hi

    for s in range(2):
        loads[near[s]].wait()
        split(S, 0, s, 0, ny)
        loads[far[s]].wait()
        residue(S, 0, s, 0, ny)

    greeted = has[0].astype(jnp.int32) + has[1].astype(jnp.int32)
    greeted = greeted + jnp.where(me == hub, half - 2, 0) + jnp.where(c == 0, n_cond - 1, 0)
    greeted = greeted + jnp.where(upper, half, 0) - jnp.where(me == half, 1, 0)
    pl.semaphore_wait(bar, greeted)
    for s in range(2):
        @pl.when(has[s])
        def _():
            piece(0, s, 0, *cuts[0][0]).start()

    for cp in small:
        cp.wait()
    entry = lax.broadcasted_iota(jnp.int32, fv.shape, 1)
    inflow = jnp.sum(jnp.where(entry == ridx[0], fv[...], 0.0), axis=1, keepdims=True)
    drift = (transport_step * inflow) * profile
    n_rows = tv.shape[0]
    match = (ov[...] == lax.broadcasted_iota(jnp.int32, (n_slab, n_rows), 0)).astype(F32)
    prior = (
        lax.broadcasted_iota(jnp.int32, (n_rows, n_rows), 0) < lax.broadcasted_iota(jnp.int32, (n_rows, n_rows), 1)
    ).astype(BF16)
    earlier = jnp.dot(match.astype(BF16), prior, preferred_element_type=F32)
    first = jnp.where(earlier < 0.5, match, 0.0)
    second = match - first
    code = cv[...].astype(F32) + 16.0
    lanes = lax.broadcasted_iota(jnp.int32, (n_slab, nz), 1)
    high = jnp.zeros((n_slab, nz), F32)
    low = jnp.zeros((n_slab, nz), F32)
    for i, pick in enumerate((first, second)):
        ST[:, i, :] = jnp.dot(pick.astype(BF16), tv[...], preferred_element_type=F32).astype(ST.dtype)
        mine = jnp.sum(pick * code, axis=1, keepdims=True)
        hi_part = jnp.floor(mine * (1.0 / 16.0))
        here = lanes == me + i * n_slab
        high = jnp.where(here, hi_part, high)
        low = jnp.where(here, mine - 16.0 * hi_part, low)
    ST[:, 2, :] = high.astype(ST.dtype)
    ST[:, 3, :] = low.astype(ST.dtype)
    RT[me] = ST[me]

    def row_copy(d, slot):
        return pltpu.make_async_remote_copy(
            src_ref=ST.at[d], dst_ref=RT.at[slot], send_sem=ts.at[d], recv_sem=tr.at[slot],
            device_id=(c, d), device_id_type=MESH,
        )

    @pl.when(upper)
    def _():
        def one(d, _):
            row_copy(d, me).start()
            return 0
        lax.fori_loop(0, half, one, 0)
    for k in range(1, CHUNKS):
        for s in range(2):
            @pl.when(has[s])
            def _():
                piece(0, s, k, *cuts[0][k]).start()

    @pl.when(me == hub)
    def _():
        def tell(i, _):
            pl.semaphore_signal(go, inc=1, device_id=(c, me - i), device_id_type=MESH)
            return 0
        lax.fori_loop(1, half, tell, 0)

    @pl.when(upper)
    def _():
        def tell(d, _):
            pl.semaphore_signal(up, inc=1, device_id=(c, d), device_id_type=MESH)
            return 0
        lax.fori_loop(0, half, tell, 0)

    @pl.when(c == 0)
    def _():
        def tell(d, _):
            pl.semaphore_signal(go2, inc=1, device_id=(d, me), device_id_type=MESH)
            return 0
        lax.fori_loop(1, n_cond, tell, 0)

    first_own = jnp.where(upper, half, 0)

    def send_own_half():
        @pl.when(me != hub)
        def _():
            pl.semaphore_wait(go, 1)

        def one(i, _):
            row_copy(first_own + lax.rem(me - first_own + i, half), me).start()
            return 0
        lax.fori_loop(1, half, one, 0)

    def send_upper():
        pl.semaphore_wait(up, n_slab - half)

        def one(d, _):
            row_copy(d, me).start()
            return 0
        lax.fori_loop(half, n_slab, one, 0)

    ghost = (has[0].astype(F32), has[1].astype(F32))

    def local_step(src, dst, padded):
        def laps(r, n):
            for j in range(nx):
                v = in_plane(src, j, r, n)
                for o in (j - 1, j + 1):
                    if 0 <= o < nx:
                        v = v + src[o, pl.ds(r + PAD, n), :]
                F[j, pl.ds(r + PAD, n), :] = v
        rows(0, ny, laps)

        def update(r, n):
            for j in range(nx):
                lap2 = in_plane(F, j, r, n)
                for o in (j - 1, j + 1):
                    if 0 <= o < nx:
                        lap2 = lap2 + F[o, pl.ds(r + PAD, n), :]
                x = src[j, pl.ds(r + PAD, n), :]
                for s in range(2):
                    if j == near[s]:
                        lap2 = lap2 + ghost[s] * x
                moved = src[j, pl.ds(r + (PAD + 1), n), :] - src[j, pl.ds(r + (PAD - 1), n), :]
                v = x + mobility(j, r, n) * F[j, pl.ds(r + PAD, n), :] - stiffness_step * lap2 + drift * moved
                dst[j, pl.ds(r + padded, n), :] = v
        rows(0, ny, update)

    def unpack(phase, s, lo, hi):
        def body(r, n):
            H[s, pl.ds(r + PAD, n), :] = RB[phase, s, 0, pl.ds(r, n), :].astype(F32)
        rows(lo, hi, body)

    def correct(phase, dst, padded, s, lo, hi):
        def body(r, n):
            h = H[s, pl.ds(r + PAD, n), :]
            v = dst[near[s], pl.ds(r + padded, n), :] + mobility(near[s], r, n) * h
            v = v - 2.0 * stiffness_step * in_plane(H, s, r, n) + RB[phase, s, 1, pl.ds(r, n), :].astype(F32)
            dst[near[s], pl.ds(r + padded, n), :] = v
            dst[far[s], pl.ds(r + padded, n), :] = dst[far[s], pl.ds(r + padded, n), :] - stiffness_step * h
        rows(lo, hi, body)

    def chosen(places):
        row = lax.broadcasted_iota(jnp.int32, (8, nz), 0)
        col = lax.broadcasted_iota(jnp.int32, (8, nz), 1)
        pick = jnp.zeros((8, nz), F32)
        for i, z in places:
            pick = jnp.where(jnp.logical_and(row == i, col == z), 1.0, pick)
        return pick

    def turned(pick, x, **kw):
        return lax.dot_general(pick, x, (((1,), (1,)), ((), ())), preferred_element_type=F32, **kw)

    pick_wall = chosen(((0, 0), (1, nz - 1)))
    pick_t = chosen(((0, 0), (1, nz - 1), (2, 1), (3, nz - 2))).astype(BF16)
    pick_q = chosen(((4, 0), (5, nz - 1))).astype(BF16)

    def wall_lanes(s):
        WS[s] = (turned(pick_t, SB[1, s, 0]) + turned(pick_q, SB[1, s, 1])).astype(BF16)

    def wall_out(s):
        return pltpu.make_async_remote_copy(
            src_ref=WS.at[s], dst_ref=WR.at[1 - s], send_sem=ws.at[s], recv_sem=wr.at[1 - s],
            device_id=(c, peer[s]), device_id_type=MESH,
        )

    def wall_in(s):
        return pltpu.make_async_remote_copy(
            src_ref=WS.at[1 - s], dst_ref=WR.at[s], send_sem=ws.at[1 - s], recv_sem=wr.at[s],
            device_id=(c, peer[s]), device_id_type=MESH,
        )

    ph_load.wait()
    local_step(S, S1, PAD)
    for k in range(CHUNKS):
        for s in range(2):
            @pl.when(has[s])
            def _():
                landing(0, s, k, *cuts[0][k]).wait_recv()
                unpack(0, s, *cuts[0][k])
                lo, hi = lagged(0, k, 16)
                correct(0, S1, PAD, s, lo, hi)
                split(S1, 1, s, lo, hi)
                residue(S1, 1, s, *cuts[1][k])
                if k < HELD:
                    piece(1, s, k, *cuts[1][k]).start()
                if k == CHUNKS - 1:
                    wall_lanes(s)
                    wall_out(s).start()
        if k == 1:
            send_own_half()

    def release(k):
        for s in range(2):
            @pl.when(has[s])
            def _():
                piece(1, s, k, *cuts[1][k]).start()

    @pl.when(jnp.logical_not(upper))
    def _():
        send_upper()

    for k in range(HELD, CHUNKS - 1):
        release(k)
    local_step(S1, OB, 0)

    lane_y = lax.broadcasted_iota(jnp.int32, (1, ny), 1)
    keep_first = (lane_y > 0).astype(F32)
    keep_last = (lane_y < ny - 1).astype(F32)
    for j in range(nx):
        both = S1[j, pl.ds(PAD, ny), :] + OB[j]
        BW[j] = turned(pick_wall, both, precision=lax.Precision.HIGHEST)[0:2, :]
        EP[j] = turned(pick_wall.astype(BF16), PB[j])[0:2, :]

    def wall_correct(s):
        w = WR[s].astype(F32)
        t, n, q = w[0:2, :], w[2:4, :], w[4:6, :]
        p = EP[near[s]]
        beside = pltpu.roll(t, 1, 1) * keep_first + pltpu.roll(t, ny - 1, 1) * keep_last
        d = ((3.0 * mobility_step) * (p * p) - mobility_step) * t + q
        d = d - 2.0 * stiffness_step * (n + beside - 6.0 * t)
        BW[near[s]] = BW[near[s]] + d
        BW[far[s]] = BW[far[s]] - stiffness_step * t

    def finish_chunk(k):
        lo, hi = lagged(1, k, 16)
        for s in range(2):
            @pl.when(has[s])
            def _():
                landing(1, s, k, *cuts[1][k]).wait_recv()
                unpack(1, s, *cuts[1][k])
                correct(1, OB, 0, s, lo, hi)

    n_red = GS.shape[0]
    stride = n_cond // n_red
    for s in range(2):
        @pl.when(has[s])
        def _():
            wall_in(s).wait_recv()
            wall_correct(s)
    for j in range(nx):
        p = EP[j]
        g = (1.0 - p * p) * BW[j]
        for w in range(2):
            GS[2 * j + w] = g[w : w + 1, :]

    @pl.when(c > 0)
    def _():
        pl.semaphore_wait(go2, 1)

    def part(r, slot):
        return pltpu.make_async_remote_copy(
            src_ref=GS.at[r], dst_ref=RR.at[slot], send_sem=gs.at[r], recv_sem=gr.at[slot],
            device_id=(r * stride, me), device_id_type=MESH,
        )

    def whole(d, r):
        return pltpu.make_async_remote_copy(
            src_ref=tot, dst_ref=FIN.at[r], send_sem=fs.at[d], recv_sem=fr.at[r],
            device_id=(d, me), device_id_type=MESH,
        )

    for r in range(n_red):
        @pl.when(c != r * stride)
        def _():
            part(r, c).start()

    mine_r = c // stride
    reducer = lax.rem(c, stride) == 0

    release(CHUNKS - 1)

    @pl.when(reducer)
    def _():
        tot[...] = GS[mine_r]

        def add(i, _):
            d = lax.rem(c + i, n_cond)
            part(mine_r, d).wait_recv()
            tot[...] = tot[...] + RR[d]
            return 0
        lax.fori_loop(1, n_cond, add, 0)

        def tell(i, _):
            whole(lax.rem(c + i, n_cond), mine_r).start()
            return 0
        lax.fori_loop(1, n_cond, tell, 0)
        FIN[mine_r] = tot[...]

    for k in range(CHUNKS - 1):
        finish_chunk(k)

    def rows_in(i, _):
        d = lax.rem(me + i, n_slab)
        row_copy(d, d).wait_recv()
        return 0
    lax.fori_loop(1, n_slab, rows_in, 0)
    TA[...] = jnp.zeros_like(TA)
    for i in range(2):
        TA[pl.ds(i * n_slab, n_slab), pl.ds(0, nz)] = RT[:, i, :].astype(BF16)
    TA[:, pl.ds(nz, nz)] = jnp.ones((nz, nz), BF16)
    hi_sum = jnp.sum(RT[:, 2, :].astype(F32), axis=0, keepdims=True)
    lo_sum = jnp.sum(RT[:, 3, :].astype(F32), axis=0, keepdims=True)
    where_to = ((hi_sum - 1.0) * 16.0 + lo_sum).astype(jnp.int32)
    per = ny // nz
    for j in range(nx):
        for b in range(per):
            r = b * nz
            at = lax.broadcasted_iota(jnp.int32, (nz, nz), 0) + (j * ny + r)
            hit = (at == where_to).astype(F32).astype(BF16)
            both = jnp.dot(hit, TA[...], preferred_element_type=F32)
            p = PB[j, pl.ds(r, nz), :].astype(F32)
            OB[j, pl.ds(r, nz), :] = OB[j, pl.ds(r, nz), :] + (p * both[:, nz:] - both[:, :nz])


    finish_chunk(CHUNKS - 1)

    for r in range(n_red):
        @pl.when(c != r * stride)
        def _():
            whole(c, r).wait_recv()
    for w in range(2):
        for x in range(nx):
            grad[w, x : x + 1, :] = (wall_weight * mv[w, x : x + 1, :].astype(F32)) * FIN[2 * x + w]

    for phase in range(2):
        for s in range(2):
            @pl.when(has[s])
            def _():
                for k in range(CHUNKS):
                    piece(phase, s, k, *cuts[phase][k]).wait_send()

    def rows_out(i, _):
        d = lax.rem(me + i, n_slab)
        row_copy(d, me).wait_send()
        return 0
    lax.fori_loop(1, n_slab, rows_out, 0)
    for r in range(n_red):
        @pl.when(c != r * stride)
        def _():
            part(r, c).wait_send()

    @pl.when(reducer)
    def _():
        def sent(i, _):
            whole(lax.rem(c + i, n_cond), mine_r).wait_send()
            return 0
        lax.fori_loop(1, n_cond, sent, 0)
    for s in range(2):
        @pl.when(has[s])
        def _():
            wall_out(s).wait_send()


def deliver(state, walls, out, grad, sem):
    ny = state.shape[2]
    parts = [
        pltpu.make_async_copy(state.at[0, j], out.at[0, j], sem.at[j]) for j in range(state.shape[1])
    ]
    parts.append(pltpu.make_async_copy(walls, grad, sem.at[state.shape[1]]))
    for cp in parts:
        cp.start()
    for cp in parts:
        cp.wait()


def on_device(adjoint, phase, targets, owners, target_cell, rate_index, inflow_rates, wall_mask):
    n_cond = lax.axis_size("cond")
    n_slab = lax.axis_size("slab")
    _, nx, ny, nz = adjoint.shape
    n_rows = targets.shape[1]
    n_red = 2 * nx
    n_rates = inflow_rates.shape[0]
    hbm = pl.BlockSpec(memory_space=pltpu.HBM)
    vmem = pl.BlockSpec(memory_space=pltpu.VMEM)
    dma = pltpu.SemaphoreType.DMA
    padded = ny + 2 * PAD
    call = pl.pallas_call(
        functools.partial(kernel, n_cond, n_slab),
        out_shape=(
            pltpu.VMEM(adjoint.shape, F32),
            pltpu.VMEM(wall_mask.shape, F32),
        ),
        in_specs=[hbm] * 5 + [pl.BlockSpec(memory_space=pltpu.SMEM)] + [hbm] * 2,
        out_specs=(vmem, vmem),
        scratch_shapes=[
            pltpu.VMEM((nx, padded, nz), F32),
            pltpu.VMEM((nx, ny, nz), BF16),
            pltpu.VMEM((nx, padded, nz), F32),
            pltpu.VMEM((nx, padded, nz), F32),
            pltpu.VMEM((2, padded, nz), F32),
            pltpu.VMEM((2, padded, nz), F32),
            pltpu.VMEM((2, 2, 2, ny, nz), BF16),
            pltpu.VMEM((2, 2, 2, ny, nz), BF16),
            pltpu.VMEM((n_rows, nz), BF16),
            pltpu.VMEM((1, n_rows), jnp.int32),
            pltpu.VMEM((1, n_rows), jnp.int32),
            pltpu.VMEM(wall_mask.shape, jnp.int32),
            pltpu.VMEM((1, n_rates), F32),
            pltpu.VMEM((n_slab, 4, nz), ROW),
            pltpu.VMEM((n_slab, 4, nz), ROW),
            pltpu.VMEM((nz, 2 * nz), BF16),
            pltpu.VMEM((nx, 2, ny), F32),
            pltpu.VMEM((nx, 2, ny), F32),
            pltpu.VMEM((2, 8, ny), BF16),
            pltpu.VMEM((2, 8, ny), BF16),
            pltpu.VMEM((n_red, 1, ny), F32),
            pltpu.VMEM((n_cond, 1, ny), F32),
            pltpu.VMEM((n_red, 1, ny), F32),
            pltpu.VMEM((1, ny), F32),
            dma((nx + 6,)),
            dma((2, 2, CHUNKS)),
            dma((2, 2, CHUNKS)),
            dma((n_slab,)),
            dma((n_slab,)),
            dma((n_red,)),
            dma((n_cond,)),
            dma((n_cond,)),
            dma((n_red,)),
            dma((2,)),
            dma((2,)),
            pltpu.SemaphoreType.REGULAR,
            pltpu.SemaphoreType.REGULAR,
            pltpu.SemaphoreType.REGULAR,
        ],
        compiler_params=pltpu.CompilerParams(
            collective_id=0, has_side_effects=True, vmem_limit_bytes=56 * 1024 * 1024
        ),
    )
    owner_row = owners.reshape(1, n_rows)
    state, walls = call(
        adjoint, phase, targets, owner_row, target_cell,
        rate_index, inflow_rates.reshape(1, n_rates), wall_mask,
    )
    return pl.pallas_call(
        deliver,
        out_shape=(
            jax.ShapeDtypeStruct(adjoint.shape, F32),
            jax.ShapeDtypeStruct(wall_mask.shape, F32),
        ),
        in_specs=[pl.BlockSpec(memory_space=pl.ANY)] * 2,
        out_specs=(hbm, hbm),
        scratch_shapes=[dma((nx + 1,))],
        compiler_params=pltpu.CompilerParams(vmem_limit_bytes=4 * 1024 * 1024),
    )(state, walls)


ROW = BF16


def solution(mesh):
    in_specs = (
        P("cond", "slab", None, None),
        P("cond", "slab", None, None),
        P("cond", "slab", None),
        P("cond", "slab", None),
        P("cond", "slab"),
        P("cond"),
        P(),
        P(None, "slab", None),
    )
    out_specs = (P("cond", "slab", None, None), P(None, "slab", None))
    return jax.shard_map(
        on_device, mesh=mesh, in_specs=in_specs, out_specs=out_specs, check_vma=False
    )
```

time: 70.4 us -> 47.6 us (0.68)
  the two profiles are of different devices: /device:TPU:569 before, /device:TPU:449 now
where the time goes in v2:
time: 47.6 us; the launch traced here: 47.4 us
  Pallas kernels  46.1 us (97%)
  between operations  1.29 us (3%)
    pallas_call x1, Pallas kernels, on_device(): call(adjoint, phase, targets, owner_row, target_cell, rate_index, inflow_...  45.1 us
    pallas_call x1, Pallas kernels, on_device(): pl.pallas_call(deliver, out_shape=(jax.ShapeDtypeStruct(adjoint.shape, F3...  1.01 us

profile of v2, /device:TPU:449, one launch (start us, length us, event | category | flops | bytes accessed | tf_op | source)
XLA Modules:
  0.0 47.4 jit_solution(13850712190508769881)
XLA Ops:
  1.3 45.1 %shard_map.95 = (f32[1,4,512,128]{3,2,1,0:T(8,128)S(1)}, f32[2,4,512]{2,1,0:T(4,128)S(1)}) custom-call(f32[1,4,512,128]{3,2,1,0:T(8,128)} %adj.1, bf16[1,4,512,128]{3,2,1,0:T(8,128)(2,1)} %ph.1, bf16[1,32,128]{2,1,0:T(8,128)(2,1)} %tgt.1, s32[1,32]{1,0:T(1,128)} %bitcast.2, s32[1,32]{1,0:T(1,128)} %cell.1, s32[1]{0:T(128)S(6)} %copy.10.ridx, ...), custom_call_target="tpu_custom_call" | custom-call | tf_op jit(solution)/shard_map/pallas_call | solution.py:589
  46.4 1.0 %shard_map.96 = (f32[1,4,512,128]{3,2,1,0:T(8,128)}, f32[2,4,512]{2,1,0:T(4,128)}) custom-call(f32[1,4,512,128]{3,2,1,0:T(8,128)S(1)} %get-tuple-element.4.state, f32[2,4,512]{2,1,0:T(4,128)S(1)} %get-tuple-element.5.walls), custom_call_target="tpu_custom_call" | custom-call | tf_op jit(solution)/shard_map/pallas_call | solution.py:593

commit v3 on v2

--- a/solution.py
+++ b/solution.py
@@ -17,7 +17,7 @@
 wall_weight = 0.25
 
 CHUNKS = 4
-HELD = 2
+HELD = 1
 PAD = 8
 
 
@@ -427,6 +427,8 @@
     reducer = lax.rem(c, stride) == 0
 
     release(CHUNKS - 1)
+    for k in range(CHUNKS - 2):
+        finish_chunk(k)
 
     @pl.when(reducer)
     def _():
@@ -445,8 +447,7 @@
         lax.fori_loop(1, n_cond, tell, 0)
         FIN[mine_r] = tot[...]
 
-    for k in range(CHUNKS - 1):
-        finish_chunk(k)
+    finish_chunk(CHUNKS - 2)
 
     def rows_in(i, _):
         d = lax.rem(me + i, n_slab)

time: 47.6 us -> 46.2 us (0.971)
  the two profiles are of different devices: /device:TPU:449 before, /device:TPU:321 now
where the time goes in v3:
time: 46.2 us; the launch traced here: 46 us
  Pallas kernels  44.7 us (97%)
  between operations  1.29 us (3%)
    pallas_call x1, Pallas kernels, on_device(): call(adjoint, phase, targets, owner_row, target_cell, rate_index, inflow_...  43.7 us
    pallas_call x1, Pallas kernels, on_device(): pl.pallas_call(deliver, out_shape=(jax.ShapeDtypeStruct(adjoint.shape, F3...  1.01 us

profile of v3, /device:TPU:321, one launch (start us, length us, event | category | flops | bytes accessed | tf_op | source)
XLA Modules:
  0.0 46.0 jit_solution(8955273159033202283)
XLA Ops:
  1.3 43.7 %shard_map.95 = (f32[1,4,512,128]{3,2,1,0:T(8,128)S(1)}, f32[2,4,512]{2,1,0:T(4,128)S(1)}) custom-call(f32[1,4,512,128]{3,2,1,0:T(8,128)} %adj.1, bf16[1,4,512,128]{3,2,1,0:T(8,128)(2,1)} %ph.1, bf16[1,32,128]{2,1,0:T(8,128)(2,1)} %tgt.1, s32[1,32]{1,0:T(1,128)} %bitcast.2, s32[1,32]{1,0:T(1,128)} %cell.1, s32[1]{0:T(128)S(6)} %copy.10.ridx, ...), custom_call_target="tpu_custom_call" | custom-call | tf_op jit(solution)/shard_map/pallas_call | solution.py:590
  45.0 1.0 %shard_map.96 = (f32[1,4,512,128]{3,2,1,0:T(8,128)}, f32[2,4,512]{2,1,0:T(4,128)}) custom-call(f32[1,4,512,128]{3,2,1,0:T(8,128)S(1)} %get-tuple-element.4.state, f32[2,4,512]{2,1,0:T(4,128)S(1)} %get-tuple-element.5.walls), custom_call_target="tpu_custom_call" | custom-call | tf_op jit(solution)/shard_map/pallas_call | solution.py:594

commit v4 on v3

--- a/solution.py
+++ b/solution.py
@@ -157,9 +157,9 @@
 
     for s in range(2):
         loads[near[s]].wait()
-        split(S, 0, s, 0, ny)
+        split(S, 0, s, 0, step + 16)
         loads[far[s]].wait()
-        residue(S, 0, s, 0, ny)
+        residue(S, 0, s, 0, step)
 
     greeted = has[0].astype(jnp.int32) + has[1].astype(jnp.int32)
     greeted = greeted + jnp.where(me == hub, half - 2, 0) + jnp.where(c == 0, n_cond - 1, 0)
@@ -169,6 +169,10 @@
         @pl.when(has[s])
         def _():
             piece(0, s, 0, *cuts[0][0]).start()
+
+    for s in range(2):
+        split(S, 0, s, step + 16, ny)
+        residue(S, 0, s, step, ny)
 
     for cp in small:
         cp.wait()

time: 46.2 us -> 46.1 us (level)
  no operation moved by 1% of the time
where the time goes in v4:
time: 46.1 us; the launch traced here: 45.9 us
  Pallas kernels  44.6 us (97%)
  between operations  1.29 us (3%)
    pallas_call x1, Pallas kernels, on_device(): call(adjoint, phase, targets, owner_row, target_cell, rate_index, inflow_...  43.6 us
    pallas_call x1, Pallas kernels, on_device(): pl.pallas_call(deliver, out_shape=(jax.ShapeDtypeStruct(adjoint.shape, F3...  1.01 us

profile of v4, /device:TPU:321, one launch (start us, length us, event | category | flops | bytes accessed | tf_op | source)
XLA Modules:
  0.0 45.9 jit_solution(2781579325353118281)
XLA Ops:
  1.3 43.6 %shard_map.95 = (f32[1,4,512,128]{3,2,1,0:T(8,128)S(1)}, f32[2,4,512]{2,1,0:T(4,128)S(1)}) custom-call(f32[1,4,512,128]{3,2,1,0:T(8,128)} %adj.1, bf16[1,4,512,128]{3,2,1,0:T(8,128)(2,1)} %ph.1, bf16[1,32,128]{2,1,0:T(8,128)(2,1)} %tgt.1, s32[1,32]{1,0:T(1,128)} %bitcast.2, s32[1,32]{1,0:T(1,128)} %cell.1, s32[1]{0:T(128)S(6)} %copy.10.ridx, ...), custom_call_target="tpu_custom_call" | custom-call | tf_op jit(solution)/shard_map/pallas_call | solution.py:594
  44.9 1.0 %shard_map.96 = (f32[1,4,512,128]{3,2,1,0:T(8,128)}, f32[2,4,512]{2,1,0:T(4,128)}) custom-call(f32[1,4,512,128]{3,2,1,0:T(8,128)S(1)} %get-tuple-element.4.state, f32[2,4,512]{2,1,0:T(4,128)S(1)} %get-tuple-element.5.walls), custom_call_target="tpu_custom_call" | custom-call | tf_op jit(solution)/shard_map/pallas_call | solution.py:598
